TPU v7x, 32 devices: a whole 2x2x4 slice. The times are simulated.
32 devices in a mesh: dp: 8 (over y, x, core), ctx: 4 (over z).
Axes of the slice: x: 2, y: 2, z: 4, core: 2. Of those that a mesh axis runs over, the one named last changes fastest.
Arguments:
- inputs: bfloat16 [4096, 8192], P('ctx', 'dp'), may hold values from -6 to 6
- cotangent: bfloat16 [4096, 8192], P('ctx', 'dp'), may hold values from -6 to 6
- residue: float32 [8192], P('dp'), may hold values from -0.6 to 0.6
- decay: float32 [8192], P('dp'), may hold values from 7.324219e-05 to 0.05
- skip_gain: float32 [8192], P('dp'), may hold values from -4 to 4
- band_blocks: int32 [8, 4], P('dp'), may hold values from 0 to 3, each once within a row
Outputs:
- layer_out: bfloat16 [4096, 8192], P('ctx', 'dp')
- input_grad: bfloat16 [4096, 8192], P('ctx', 'dp')
- skip_grad: float32 [8192], P(('dp', 'ctx'))
- residue_grad: float32 [8192], P(('dp', 'ctx'))
- decay_grad: float32 [8192], P(('dp', 'ctx'))
Inputs may be any that keep to these rules, and one draw needn't show every extreme that they name: Each row of band_blocks holds each of 0 to 3 exactly once.
All inputs are finite; a program needn't handle non-finite values.
Results may differ from a plain program's by a relative error of at most 0.0019.
Values may be sent and summed in bfloat16 or wider, within the bound.
A program may use at most 128 MiB of HBM per device.

v0:
```python
import jax
import jax.numpy as jnp
from jax import lax
from jax.sharding import PartitionSpec as P


def prefix(value, axis, join, neutral, backward):
    count, mine = (lax.axis_size(axis), lax.axis_index(axis))
    pieces = jax.tree.map(lambda part: lax.all_gather(part, axis), value)
    if backward:
        pieces = jax.tree.map(lambda part: part[::-1], pieces)
        mine = count - 1 - mine
    total = jax.tree.map(
        lambda part, zero: jnp.full_like(part, 0) + jnp.asarray(zero, part.dtype), value, neutral
    )

    def turn(position, total):
        longer = join(total, jax.tree.map(lambda part: part[position], pieces))
        return jax.tree.map(lambda new, old: jnp.where(position < mine, new, old), longer, total)

    return lax.fori_loop(0, count - 1, turn, total)


def compose(earlier_pair, later_pair):
    return (earlier_pair[0] * later_pair[0], earlier_pair[1] * later_pair[0] + later_pair[1])


def chain_step(earlier_pair, later_pair):
    return (earlier_pair[0] * later_pair[1] + later_pair[0], earlier_pair[1] * later_pair[1])


def local_scan(values, decay_rate, backward):
    factors = jnp.broadcast_to(jnp.exp(-decay_rate)[None, :], values.shape)
    return lax.associative_scan(compose, (factors, values), reverse=backward)[1]


def slot_groups(bands, ctx_rank, direction):
    group_count = bands.shape[0]
    slot_index = jnp.arange(group_count, dtype=jnp.int32)
    distance = (slot_index - ctx_rank) * direction
    matches = bands[None, :] + 1 == distance[:, None]
    return jnp.sum(jnp.where(matches, slot_index[None, :], 0), axis=1)


def outgoing(values, slot_group, group_count, group_width):
    shaped = values.reshape(values.shape[0], group_count, group_width)
    return jnp.take(shaped, slot_group, axis=1)


def incoming(received, source, in_range):
    picked = jnp.take(received, source, axis=1)
    picked = jnp.where(in_range[None, :, None], picked, jnp.zeros((), picked.dtype))
    return picked.reshape(picked.shape[0], -1)


def body(inputs, cotangent, residue, decay, skip_gain, band_blocks):
    values = inputs.astype(jnp.float32)
    upstream = cotangent.astype(jnp.float32)
    bands = band_blocks[0]
    block_rows, channels = values.shape
    group_count = bands.shape[0]
    group_width = channels // group_count
    ctx_rank = lax.axis_index("ctx")
    offsets = jnp.arange(block_rows, dtype=jnp.float32)[:, None]
    lengths = jnp.repeat(
        (bands + 1) * block_rows, group_width, total_repeat_length=channels
    ).astype(jnp.float32)
    band_tail = jnp.exp(-decay * lengths)[None, :]
    block_decay = jnp.exp(-decay * block_rows)
    lead_decay = jnp.exp(-decay[None, :] * (offsets + 1.0))
    trail_decay = jnp.exp(-decay[None, :] * (block_rows - offsets))
    zero_state = jnp.zeros_like(decay)
    unit_state = jnp.ones_like(decay)
    inside = local_scan(values, decay, False)
    before, _ = prefix(
        (inside[-1], block_decay), "ctx", chain_step, (zero_state, unit_state), False
    )
    carried = inside + lead_decay * before[None, :]
    send_fwd = slot_groups(bands, ctx_rank, 1)
    source_fwd = ctx_rank - bands - 1
    valid_fwd = source_fwd >= 0
    source_fwd = jnp.clip(source_fwd, 0, group_count - 1)
    inside_back = local_scan(upstream, decay, True)
    after, _ = prefix(
        (inside_back[0], block_decay), "ctx", chain_step, (zero_state, unit_state), True
    )
    back_carried = inside_back + trail_decay * after[None, :]
    send_bwd = slot_groups(bands, ctx_rank, -1)
    source_bwd = ctx_rank + bands + 1
    valid_bwd = source_bwd < group_count
    source_bwd = jnp.clip(source_bwd, 0, group_count - 1)
    received = lax.all_to_all(
        outgoing(carried, send_fwd, group_count, group_width),
        "ctx",
        split_axis=1,
        concat_axis=1,
        tiled=True,
    )
    far_state = incoming(received, source_fwd, valid_fwd)
    received_back = lax.all_to_all(
        outgoing(back_carried, send_bwd, group_count, group_width),
        "ctx",
        split_axis=1,
        concat_axis=1,
        tiled=True,
    )
    near_state = incoming(received_back, source_bwd, valid_bwd)
    truncated = carried - band_tail * far_state
    layer_out = (skip_gain[None, :] * values + residue[None, :] * truncated).astype(jnp.bfloat16)
    back_truncated = back_carried - band_tail * near_state
    input_grad = (skip_gain[None, :] * upstream + residue[None, :] * back_truncated).astype(
        jnp.bfloat16
    )
    position = ctx_rank.astype(jnp.float32) * block_rows + offsets
    weighted = upstream * truncated
    moment = jnp.sum(position * weighted, axis=0) - jnp.sum(
        position * values * back_truncated, axis=0
    )
    grad_terms = jnp.stack(
        [jnp.sum(values * upstream, axis=0), jnp.sum(weighted, axis=0), -decay * residue * moment]
    )
    share_width = channels // lax.axis_size("ctx")
    summed = lax.psum(grad_terms, "ctx")
    own_share = lax.dynamic_slice_in_dim(summed, ctx_rank * share_width, share_width, 1)
    return (layer_out, input_grad, own_share[0], own_share[1], own_share[2])


def solution(mesh):
    placed = (P("ctx", "dp"), P("ctx", "dp"), P("dp"), P("dp"), P("dp"), P("dp", None))
    return jax.shard_map(
        body,
        mesh=mesh,
        in_specs=placed,
        out_specs=(
            P("ctx", "dp"),
            P("ctx", "dp"),
            P(("dp", "ctx")),
            P(("dp", "ctx")),
            P(("dp", "ctx")),
        ),
        check_vma=False,
    )
```

profile of v0, /device:TPU:0, one launch (start us, length us, event | category | flops | bytes accessed | tf_op | source)
XLA Modules:
  0.0 798.9 jit_solution(3415953505581244553)
XLA Ops:
  0.7 9.8 %slice.553 = f32[512,1024]{1,0:T(8,128)} slice(bf16[1024,1024]{1,0:T(8,128)(2,1)} %param.15), slice={[1:1024:2], [0:1024:1]} | slice | bytes 4194304 | tf_op jit(solution)/shard_map/slice | solution.py:34
  10.5 5.7 slice.556
  22.8 16.6 %slice.555 = f32[512,1024]{1,0:T(8,128)} reverse(f32[512,1024]{1,0:T(8,128)} %slice.487), dimensions={0} | reverse | bytes 4194304 | tf_op jit(solution)/shard_map/slice | solution.py:34
  39.4 16.7 %slice.554 = f32[512,1024]{1,0:T(8,128)} reverse(f32[512,1024]{1,0:T(8,128)} %slice.553), dimensions={0} | reverse | bytes 4194304 | tf_op jit(solution)/shard_map/slice | solution.py:34
  56.1 16.6 %slice.557 = f32[512,1024]{1,0:T(8,128)} reverse(f32[512,1024]{1,0:T(8,128)} %slice.556), dimensions={0} | reverse | bytes 4194304 | tf_op jit(solution)/shard_map/slice | solution.py:34
  72.7 6.0 multiply_add_fusion.2
  231.6 16.6 %pad.164 = f32[1024,1024]{1,0:T(8,128)} pad(f32[512,1024]{1,0:T(8,128)} %add.477, f32[]{:T(128)} %constant.166.clone.1), padding=1_0_1x0_0_0 | pad | bytes 6291460 | tf_op jit(solution)/shard_map/pad | solution.py:34
  249.7 17.2 %slice.626 = f32[511,1024]{1,0:T(8,128)} reverse(f32[511,1024]{1,0:T(8,128)} %slice.549), dimensions={0} | reverse | bytes 4186112 | tf_op jit(solution)/shard_map/slice | solution.py:34
  266.9 17.1 %slice.628 = f32[511,1024]{1,0:T(8,128)} reverse(f32[511,1024]{1,0:T(8,128)} %slice.627), dimensions={0} | reverse | bytes 4186112 | tf_op jit(solution)/shard_map/slice | solution.py:34
  288.1 8.9 %pad.163 = f32[1024,1024]{1,0:T(8,128)} pad(f32[512,1024]{1,0:T(8,128)S(1)} %pad_maximum_fusion.1, f32[]{:T(128)} %constant.166.clone.1), padding=0_1_1x0_0_0 | pad | bytes 6291460 | tf_op jit(solution)/shard_map/pad | solution.py:34
  298.4 6.9 add.479
  372.4 6.0 slice.550
  381.4 14.9 %all-gather.2 = f32[4,1,1024]{2,1,0:T(1,128)S(1)} all-gather(f32[1,1,1024]{2,1,0:T(1,128)S(1)} %copy-done.41), channel_id=1, replica_groups=mesh['dp'=8,'ctx'=4] {'ctx'}, dimensions={0}, use_global_device_ids=true | all-gather | bytes 20480 | tf_op jit(solution)/shard_map/all_gather | solution.py:9
  396.5 13.2 %all-gather = f32[4096]{0:T(1024)S(1)} all-gather(f32[1024]{0:T(1024)S(1)} %copy-done.40), channel_id=2, replica_groups=mesh['dp'=8,'ctx'=4] {'ctx'}, dimensions={0}, use_global_device_ids=true | all-gather | bytes 20480 | tf_op jit(solution)/shard_map/all_gather | solution.py:9
  410.4 32.8 %rev.11 = f32[1024,1024]{1,0:T(8,128)} reverse(f32[1024,1024]{1,0:T(8,128)} %add.479), dimensions={0} | reverse | bytes 8388608 | tf_op jit(solution)/shard_map/rev | solution.py:34
  461.2 8.7 %pad.141 = f32[512,1024]{1,0:T(8,128)} pad(f32[256,1024]{1,0:T(8,128)} %pad_maximum_fusion.2, f32[]{:T(128)} %constant.166.clone.1), padding=0_1_1x0_0_0 | pad | bytes 3145732 | tf_op jit(solution)/shard_map/pad | solution.py:34
  478.8 16.6 %pad.144 = f32[1024,1024]{1,0:T(8,128)} pad(f32[512,1024]{1,0:T(8,128)} %add.443, f32[]{:T(128)} %constant.166.clone.1), padding=1_0_1x0_0_0 | pad | bytes 6291460 | tf_op jit(solution)/shard_map/pad | solution.py:34
  500.5 16.7 %pad.143 = f32[1024,1024]{1,0:T(8,128)} pad(f32[512,1024]{1,0:T(8,128)} %pad_maximum_fusion, f32[]{:T(128)} %constant.166.clone.1), padding=0_1_1x0_0_0 | pad | bytes 6291460 | tf_op jit(solution)/shard_map/pad | solution.py:34
  518.0 13.2 %all-gather.1 = f32[4,1,1024]{2,1,0:T(1,128)S(1)} all-gather(f32[1,1,1024]{2,1,0:T(1,128)S(1)} %add_bitcast_fusion.1), channel_id=1, replica_groups=mesh['dp'=8,'ctx'=4] {'ctx'}, dimensions={0}, use_global_device_ids=true | all-gather | bytes 20480 | tf_op jit(solution)/shard_map/all_gather | solution.py:9
  531.4 7.6 multiply_add_fusion.1
  584.9 64.4 %all-to-all-done = f32[1024,4,256]{2,0,1:T(8,128)} async-done(((f32[1024,4,256]{2,0,1:T(8,128)}), f32[1024,4,256]{2,0,1:T(8,128)}, u32[]{:S(2)}, u32[]{:S(2)}) %all-to-all-start) | async-done | bytes 4194336 | tf_op jit(solution)/shard_map/all_to_all | solution.py:92
  674.9 71.9 %all-to-all-done.1 = f32[1024,4,256]{2,0,1:T(8,128)} async-done(((f32[1024,4,256]{2,0,1:T(8,128)}), f32[1024,4,256]{2,0,1:T(8,128)}, u32[]{:S(2)}, u32[]{:S(2)}) %all-to-all-start.1) | async-done | bytes 4194336 | tf_op jit(solution)/shard_map/all_to_all | solution.py:100
  767.3 9.8 %multiply_reduce_fusion.2 = (f32[1024]{0:T(1024)S(1)}, f32[1024]{0:T(1024)S(1)}, f32[1024]{0:T(1024)S(1)}, f32[1024]{0:T(1024)S(1)}, f32[1024,1024]{1,0:T(8,128)}, /*index=5*/bf16[1024,1024]{1,0:T(8,128)(2,1)}) fusion(bf16[1024,1024]{1,0:T(8,128)(2,1)} %param.15, bf16[1024,1024]{1,0:T(8,128)(2,1)S(1)} %copy-done, f32[1024,1024]{1,0:T(8,128)} %get-tuple-element.315, ...), kind=kLoop, calls=%fused_computation.16 | loop fusion | flops 19918848 | bytes 27295744 | tf_op jit(solution)/shard_map/reduce_sum | solution.py:120
  777.1 16.9 %psum.7 = f32[3,1024]{1,0:T(4,128)S(1)} all-reduce(f32[3,1024]{1,0:T(4,128)S(1)} %pad_maximum_fusion.16), channel_id=1, replica_groups=mesh['dp'=8,'ctx'=4] {'ctx'}, use_global_device_ids=true, to_apply=%region_10.12 | all-reduce | flops 3072 | bytes 24576 | tf_op jit(solution)/shard_map/psum | solution.py:123
  (370 shorter events, 366.3 us)
Async XLA Ops:
  333.5 33.3 %copy-start.2 = (f32[256,1024]{1,0:T(8,128)}, f32[256,1024]{1,0:T(8,128)S(1)}, u32[]{:S(2)}) copy-start(f32[256,1024]{1,0:T(8,128)S(1)} %multiply_add_fusion.5) | copy-start | bytes 3145732
  343.1 35.2 %copy-start.7 = (f32[64,1024]{1,0:T(8,128)}, f32[64,1024]{1,0:T(8,128)S(1)}, u32[]{:S(2)}) copy-start(f32[64,1024]{1,0:T(8,128)S(1)} %multiply_add_fusion.9) | copy-start | bytes 786436
  345.6 32.8 %copy-start.10 = (f32[32,1024]{1,0:T(8,128)}, f32[32,1024]{1,0:T(8,128)S(1)}, u32[]{:S(2)}) copy-start(f32[32,1024]{1,0:T(8,128)S(1)} %multiply_add_fusion.11) | copy-start | bytes 393220
  410.2 33.0 %copy-start.25 = (f32[1024]{0:T(1024)S(1)}, f32[1024]{0:T(1024)}, u32[]{:S(2)}) copy-start(f32[1024]{0:T(1024)} %get-tuple-element.321) | copy-start | bytes 12292
  410.2 33.0 %copy-start.28 = (f32[2,1024]{1,0:T(2,128)S(1)}, f32[2,1024]{1,0:T(2,128)}, u32[]{:S(2)}) copy-start(f32[2,1024]{1,0:T(2,128)} %slice.518) | copy-start | bytes 24580
  410.2 33.0 %copy-start.29 = (f32[2,1024]{1,0:T(2,128)S(1)}, f32[2,1024]{1,0:T(2,128)}, u32[]{:S(2)}) copy-start(f32[2,1024]{1,0:T(2,128)} %slice.520) | copy-start | bytes 24580
  410.2 33.0 %copy-start.39 = (f32[1024]{0:T(1024)S(1)}, f32[1024]{0:T(1024)}, u32[]{:S(2)}) copy-start(f32[1024]{0:T(1024)} %get-tuple-element.316) | copy-start | bytes 12292
  410.2 33.1 %copy-start.14 = (f32[4,1024]{1,0:T(4,128)S(1)}, f32[4,1024]{1,0:T(4,128)}, u32[]{:S(2)}) copy-start(f32[4,1024]{1,0:T(4,128)} %multiply_add_fusion.17) | copy-start | bytes 49156
  410.2 33.1 %copy-start.17 = (f32[3,1024]{1,0:T(4,128)S(1)}, f32[3,1024]{1,0:T(4,128)}, u32[]{:S(2)}) copy-start(f32[3,1024]{1,0:T(4,128)} %slice.529) | copy-start | bytes 36868
  410.2 33.1 %copy-start.26 = (f32[1024]{0:T(1024)S(1)}, f32[1024]{0:T(1024)}, u32[]{:S(2)}) copy-start(f32[1024]{0:T(1024)} %get-tuple-element.319) | copy-start | bytes 12292
  410.3 33.2 %slice-start.6 = ((f32[8,1024]{1,0:T(8,128)}), f32[1,1024]{1,0:T(1,128)S(1)}, s32[]{:S(2)}) async-start(f32[8,1024]{1,0:T(8,128)} %multiply_add_fusion.15), calls=%async_computation.8 | async-start | bytes 8192 | tf_op jit(solution)/shard_map/slice | solution.py:34
  410.3 33.3 %copy-start.13 = (f32[7,1024]{1,0:T(8,128)S(1)}, f32[7,1024]{1,0:T(8,128)}, u32[]{:S(2)}) copy-start(f32[7,1024]{1,0:T(8,128)} %slice.532) | copy-start | bytes 86020
  410.3 33.3 %copy-start.24 = (f32[1024]{0:T(1024)S(1)}, f32[1024]{0:T(1024)}, u32[]{:S(2)}) copy-start(f32[1024]{0:T(1024)} %get-tuple-element.320) | copy-start | bytes 12292
  410.3 33.3 %slice-start.5 = ((f32[16,1024]{1,0:T(8,128)}), f32[1,1024]{1,0:T(1,128)S(1)}, s32[]{:S(2)}) async-start(f32[16,1024]{1,0:T(8,128)} %multiply_add_fusion.13), calls=%async_computation.7 | async-start | bytes 8192 | tf_op jit(solution)/shard_map/slice | solution.py:34
  410.3 33.3 %copy-start.12 = (f32[15,1024]{1,0:T(8,128)S(1)}, f32[15,1024]{1,0:T(8,128)}, u32[]{:S(2)}) copy-start(f32[15,1024]{1,0:T(8,128)} %slice.535) | copy-start | bytes 184324
  410.3 33.3 %copy-start.23 = (f32[1024]{0:T(1024)S(1)}, f32[1024]{0:T(1024)}, u32[]{:S(2)}) copy-start(f32[1024]{0:T(1024)} %get-tuple-element.318) | copy-start | bytes 12292
  410.3 33.4 %slice-start.4 = ((f32[32,1024]{1,0:T(8,128)}), f32[1,1024]{1,0:T(1,128)S(1)}, s32[]{:S(2)}) async-start(f32[32,1024]{1,0:T(8,128)} %copy-done.10), calls=%async_computation.6 | async-start | bytes 8192 | tf_op jit(solution)/shard_map/slice | solution.py:34
  410.3 33.5 %copy-start.11 = (f32[31,1024]{1,0:T(8,128)S(1)}, f32[31,1024]{1,0:T(8,128)}, u32[]{:S(2)}) copy-start(f32[31,1024]{1,0:T(8,128)} %slice.538) | copy-start | bytes 380932
  410.3 33.5 %copy-start.22 = (f32[1024]{0:T(1024)S(1)}, f32[1024]{0:T(1024)}, u32[]{:S(2)}) copy-start(f32[1024]{0:T(1024)} %get-tuple-element.317) | copy-start | bytes 12292
  410.3 33.5 %slice-start.3 = ((f32[64,1024]{1,0:T(8,128)}), f32[1,1024]{1,0:T(1,128)S(1)}, s32[]{:S(2)}) async-start(f32[64,1024]{1,0:T(8,128)} %copy-done.7), calls=%async_computation.5 | async-start | bytes 8192 | tf_op jit(solution)/shard_map/slice | solution.py:34
  500.5 30.9 %copy-start.33 = (f32[1024]{0:T(1024)S(1)}, f32[1024]{0:T(1024)}, u32[]{:S(2)}) copy-start(f32[1024]{0:T(1024)} %get-tuple-element.342) | copy-start | bytes 12292
  559.6 89.7 %all-to-all-start = ((f32[1024,4,256]{2,0,1:T(8,128)}), f32[1024,4,256]{2,0,1:T(8,128)}, u32[]{:S(2)}, u32[]{:S(2)}) async-start(f32[1024,4,256]{2,0,1:T(8,128)} %select_bitcast_fusion.1), calls=%async_computation | async-start | bytes 8388608 | tf_op jit(solution)/shard_map/all_to_all | solution.py:92
  584.9 69.5 %copy-start.46 = (s32[1,4]{1,0:T(1,128)S(1)}, s32[1,4]{1,0:T(1,128)}, u32[]{:S(2)}) copy-start(s32[1,4]{1,0:T(1,128)} %param.19) | copy-start | bytes 52
  649.3 97.6 %all-to-all-start.1 = ((f32[1024,4,256]{2,0,1:T(8,128)}), f32[1024,4,256]{2,0,1:T(8,128)}, u32[]{:S(2)}, u32[]{:S(2)}) async-start(f32[1024,4,256]{2,0,1:T(8,128)} %select_bitcast_fusion), calls=%async_computation.1 | async-start | bytes 8388608 | tf_op jit(solution)/shard_map/all_to_all | solution.py:100
  (39 other events, 389.9 us)
where the time goes:
time: 814 us; the launch traced here: 799 us
  local copies, waits for them, and re-layouts  458 us (56%)
  waiting for transfers between devices  136 us (17%)
  other arithmetic  135 us (17%)
  blocking collectives  58.2 us (7%)
  starting transfers between devices  9.93 us (1%)
    slice x105, local copies, waits for them, and re-layouts, local_scan(): return lax.associative_scan(compose, (factors, values), reverse=backward)[1]  264 us
    pad x36, local copies, waits for them, and re-layouts, local_scan(): return lax.associative_scan(compose, (factors, values), reverse=backward)[1]  93.8 us
    all_to_all x1, waiting for transfers between devices, body(): lax.all_to_all(outgoing(back_carried, send_bwd, group_count, group_width)...  71.9 us
    all_to_all x1, waiting for transfers between devices, body(): lax.all_to_all(outgoing(carried, send_fwd, group_count, group_width), 'ct...  64.4 us
    all_gather x3, blocking collectives, prefix(): pieces = jax.tree.map(lambda part: lax.all_gather(part, axis), value)  41.3 us
    add x27, other arithmetic, compose(): earlier_pair[1] * later_pair[0] + later_pair[1]  38.2 us
    rev x1, local copies, waits for them, and re-layouts, local_scan(): return lax.associative_scan(compose, (factors, values), reverse=backward)[1]  32.8 us
    add x19, other arithmetic, local_scan(): return lax.associative_scan(compose, (factors, values), reverse=backward)[1]  21.3 us
  transfers between devices with their start and end apart: 2, of which 2 were waited for; matrix products, arithmetic and copies ran while one was open for 5% of the time, Pallas kernels for 0%

commit v1 on v0

--- a/solution.py
+++ b/solution.py
@@ -1,6 +1,9 @@
+import functools
 import jax
 import jax.numpy as jnp
 from jax import lax
+from jax.experimental import pallas as pl
+from jax.experimental.pallas import tpu as pltpu
 from jax.sharding import PartitionSpec as P
 
 
@@ -125,10 +128,377 @@
     return (layer_out, input_grad, own_share[0], own_share[1], own_share[2])
 
 
+MESH = pl.DeviceIdType.MESH
+LANES = 128
+ROWS = 8
+
+
+def greet(count, me):
+    barrier = pltpu.get_barrier_semaphore()
+    for step in range(1, count):
+        pl.semaphore_signal(
+            barrier,
+            inc=1,
+            device_id={"ctx": lax.rem(me + step, count)},
+            device_id_type=MESH,
+        )
+    pl.semaphore_wait(barrier, count - 1)
+
+
+def pack_kernel(bands_ref, x_ref, c_ref, decay_ref, xs_ref, cs_ref, ends_ref):
+    del bands_ref
+    rows, width = x_ref.shape
+    xs_ref[0] = x_ref[...]
+    cs_ref[0] = c_ref[...]
+    rate = decay_ref[...]
+    level = lax.broadcasted_iota(jnp.int32, (ROWS, width), 0).astype(jnp.float32)
+    leap = jnp.broadcast_to(jnp.exp(-rate * (2 * ROWS)), (ROWS, width))
+    steps = rows // (2 * ROWS)
+
+    def turn(step, sums):
+        ahead = x_ref[pl.ds(pl.multiple_of(step * 2 * ROWS, 2 * ROWS), 2 * ROWS), :]
+        back = c_ref[
+            pl.ds(pl.multiple_of((steps - 1 - step) * 2 * ROWS, 2 * ROWS), 2 * ROWS), :
+        ]
+        ahead = ahead.astype(jnp.float32)
+        back = back.astype(jnp.float32)
+        return (
+            sums[0] * leap + ahead[:ROWS],
+            sums[1] * leap + ahead[ROWS:],
+            sums[2] * leap + back[:ROWS],
+            sums[3] * leap + back[ROWS:],
+        )
+
+    zero = jnp.zeros((ROWS, width), jnp.float32)
+    upper, lower, back_upper, back_lower = lax.fori_loop(
+        0, steps, turn, (zero, zero, zero, zero), unroll=4
+    )
+    last = upper * jnp.exp(-rate * (2 * ROWS - 1 - level)) + lower * jnp.exp(
+        -rate * (ROWS - 1 - level)
+    )
+    first = back_upper * jnp.exp(-rate * level) + back_lower * jnp.exp(-rate * (ROWS + level))
+    ends_ref[0:1, :] = jnp.sum(last, axis=0, keepdims=True)
+    ends_ref[1:2, :] = jnp.sum(first, axis=0, keepdims=True)
+
+
+def pack(bands, inputs, cotangent, decay):
+    rows, channels = inputs.shape
+    groups = bands.shape[0]
+    width = channels // groups
+    block = pl.BlockSpec((rows, width), lambda g, bands: (0, g))
+    slot = pl.BlockSpec((1, rows, width), lambda g, bands: (bands[g], 0, 0))
+    return pl.pallas_call(
+        pack_kernel,
+        grid_spec=pltpu.PrefetchScalarGridSpec(
+            num_scalar_prefetch=1,
+            grid=(groups,),
+            in_specs=[block, block, pl.BlockSpec((1, width), lambda g, bands: (0, g))],
+            out_specs=[slot, slot, pl.BlockSpec((2, width), lambda g, bands: (0, g))],
+        ),
+        out_shape=(
+            jax.ShapeDtypeStruct((groups, rows, width), inputs.dtype),
+            jax.ShapeDtypeStruct((groups, rows, width), inputs.dtype),
+            jax.ShapeDtypeStruct((2, channels), jnp.float32),
+        ),
+        name="pack",
+    )(bands, inputs, cotangent, decay)
+
+
+def swap_kernel(
+    count, xs, cs, ends, far_x, far_c, far_ends, x_send, x_recv, c_send, c_recv, e_send, e_recv
+):
+    me = lax.axis_index("ctx")
+    greet(count, me)
+
+    def end_copy(step):
+        return pltpu.make_async_remote_copy(
+            src_ref=ends,
+            dst_ref=far_ends.at[me],
+            send_sem=e_send.at[step],
+            recv_sem=e_recv.at[step],
+            device_id={"ctx": lax.rem(me + step + 1, count)},
+            device_id_type=MESH,
+        )
+
+    def x_copy(slot):
+        return pltpu.make_async_remote_copy(
+            src_ref=xs.at[slot],
+            dst_ref=far_x.at[slot],
+            send_sem=x_send.at[slot],
+            recv_sem=x_recv.at[slot],
+            device_id={"ctx": lax.rem(me + slot + 1, count)},
+            device_id_type=MESH,
+        )
+
+    def c_copy(slot):
+        return pltpu.make_async_remote_copy(
+            src_ref=cs.at[slot],
+            dst_ref=far_c.at[slot],
+            send_sem=c_send.at[slot],
+            recv_sem=c_recv.at[slot],
+            device_id={"ctx": lax.rem(me + count - slot - 1, count)},
+            device_id_type=MESH,
+        )
+
+    for step in range(count - 1):
+        end_copy(step).start()
+    for slot in range(count - 1):
+        hop = slot + 1
+        pl.when(me + hop < count)(lambda: x_copy(slot).start())
+        pl.when(me >= hop)(lambda: c_copy(slot).start())
+    for step in range(count - 1):
+        end_copy(step).wait()
+    for slot in range(count - 1):
+        hop = slot + 1
+
+        @pl.when(me + hop < count)
+        def _():
+            x_copy(slot).wait_send()
+            c_copy(slot).wait_recv()
+
+        @pl.when(me >= hop)
+        def _():
+            c_copy(slot).wait_send()
+            x_copy(slot).wait_recv()
+
+
+def swap(count, xs, cs, ends):
+    groups, rows, width = xs.shape
+    far = jax.ShapeDtypeStruct((count - 1, rows, width), xs.dtype)
+    anywhere = pl.BlockSpec(memory_space=pl.ANY)
+    one = pltpu.SemaphoreType.DMA((count - 1,))
+    return pl.pallas_call(
+        functools.partial(swap_kernel, count),
+        in_specs=[anywhere] * 3,
+        out_specs=[anywhere] * 3,
+        out_shape=(far, far, jax.ShapeDtypeStruct((count,) + ends.shape, ends.dtype)),
+        scratch_shapes=[one] * 6,
+        compiler_params=pltpu.CompilerParams(collective_id=0, has_side_effects=True),
+        name="swap",
+    )(xs, cs, ends)
+
+
+def finish_kernel(
+    count,
+    tiles_wide,
+    bands_ref,
+    x_ref,
+    c_ref,
+    far_x_ref,
+    far_c_ref,
+    ends_ref,
+    residue_ref,
+    decay_ref,
+    skip_ref,
+    out_ref,
+    grad_ref,
+    sums_ref,
+):
+    me = lax.axis_index("ctx")
+    band = bands_ref[pl.program_id(0)] + 1
+    rows, width = x_ref.shape
+    has_before = me >= band
+    has_after = me + band < count
+    rate = decay_ref[...]
+    shape = (ROWS, width)
+    carry = jnp.zeros((1, width), jnp.float32)
+    back_carry = carry
+    for other in range(count):
+        apart = me - 1 - other
+        kept = jnp.logical_and(apart >= 0, apart < band)
+        factor = jnp.exp(-rate * (jnp.maximum(apart, 0) * rows).astype(jnp.float32))
+        carry = carry + jnp.where(kept, factor * ends_ref[other, 0:1, :], 0.0)
+        apart = other - me - 1
+        kept = jnp.logical_and(apart >= 0, apart < band)
+        factor = jnp.exp(-rate * (jnp.maximum(apart, 0) * rows).astype(jnp.float32))
+        back_carry = back_carry + jnp.where(kept, factor * ends_ref[other, 1:2, :], 0.0)
+    tail = jnp.broadcast_to(jnp.exp(-rate * (band * rows).astype(jnp.float32)), shape)
+    level = lax.broadcasted_iota(jnp.int32, shape, 0)
+    depth = level.astype(jnp.float32)
+    fwd = [
+        (hop, jnp.where(level >= hop, jnp.exp(-rate * hop), 0.0)) for hop in (1, 2, 4)
+    ]
+    bwd = [
+        (ROWS - hop, jnp.where(level < ROWS - hop, jnp.exp(-rate * hop), 0.0))
+        for hop in (1, 2, 4)
+    ]
+    lead = jnp.exp(-rate * (depth + 1.0))
+    trail = jnp.exp(-rate * (ROWS - depth))
+    leap = jnp.broadcast_to(jnp.exp(-rate * ROWS), shape)
+    residue = jnp.broadcast_to(residue_ref[...], shape)
+    skip = jnp.broadcast_to(skip_ref[...], shape)
+    steps = rows // (2 * ROWS)
+
+    def scan(tile, hops):
+        for hop, factor in hops:
+            tile = tile + factor * pltpu.roll(tile, hop, 0)
+        return tile
+
+    def turn(step, state):
+        carry, back_carry, s_skip, s_w, s_tw, s_v, s_tv = state
+        at = pl.ds(pl.multiple_of(step * 2 * ROWS, 2 * ROWS), 2 * ROWS)
+        base = (step * (2 * ROWS)).astype(jnp.float32)
+        x = x_ref[at, :].astype(jnp.float32)
+        c = c_ref[at, :].astype(jnp.float32)
+        far = far_x_ref[0, at, :].astype(jnp.float32)
+        outs = []
+        for half in range(2):
+            part = slice(half * ROWS, (half + 1) * ROWS)
+            local = scan(
+                x[part] - jnp.where(has_before, tail * far[part], 0.0), fwd
+            )
+            truncated = local + lead * carry
+            carry = leap * carry + jnp.broadcast_to(local[ROWS - 1 :], shape)
+            outs.append(skip * x[part] + residue * truncated)
+            w = c[part] * truncated
+            s_skip = s_skip + x[part] * c[part]
+            s_w = s_w + w
+            s_tw = s_tw + (base + half * ROWS) * w
+        out_ref[at, :] = jnp.concatenate(outs, axis=0).astype(out_ref.dtype)
+        at = pl.ds(pl.multiple_of((steps - 1 - step) * 2 * ROWS, 2 * ROWS), 2 * ROWS)
+        base = ((steps - 1 - step) * (2 * ROWS)).astype(jnp.float32)
+        x = x_ref[at, :].astype(jnp.float32)
+        c = c_ref[at, :].astype(jnp.float32)
+        far = far_c_ref[0, at, :].astype(jnp.float32)
+        outs = [None, None]
+        for half in (1, 0):
+            part = slice(half * ROWS, (half + 1) * ROWS)
+            local = scan(c[part] - jnp.where(has_after, tail * far[part], 0.0), bwd)
+            truncated = local + trail * back_carry
+            back_carry = leap * back_carry + jnp.broadcast_to(local[:1], shape)
+            outs[half] = skip * c[part] + residue * truncated
+            v = x[part] * truncated
+            s_v = s_v + v
+            s_tv = s_tv + (base + half * ROWS) * v
+        grad_ref[at, :] = jnp.concatenate(outs, axis=0).astype(grad_ref.dtype)
+        return carry, back_carry, s_skip, s_w, s_tw, s_v, s_tv
+
+    zero = jnp.zeros(shape, jnp.float32)
+    state = (
+        jnp.broadcast_to(carry, shape),
+        jnp.broadcast_to(back_carry, shape),
+        zero,
+        zero,
+        zero,
+        zero,
+        zero,
+    )
+    _, _, s_skip, s_w, s_tw, s_v, s_tv = lax.fori_loop(0, steps, turn, state, unroll=4)
+    offset = depth + (me * rows).astype(jnp.float32)
+    moment = (s_tw - s_tv) + offset * (s_w - s_v)
+    sums_ref[0, 0:1, :] = jnp.sum(s_skip, axis=0, keepdims=True)
+    sums_ref[0, 1:2, :] = jnp.sum(s_w, axis=0, keepdims=True)
+    sums_ref[0, 2:3, :] = (
+        -rate * residue_ref[...] * jnp.sum(moment, axis=0, keepdims=True)
+    )
+
+
+def finish(count, bands, x, c, far_x, far_c, ends, residue, decay, skip):
+    rows, channels = x.shape
+    groups = bands.shape[0]
+    wide = channels // groups // LANES
+    block = pl.BlockSpec((rows, LANES), lambda g, l, bands: (0, g * wide + l))
+    far = pl.BlockSpec(
+        (1, rows, LANES), lambda g, l, bands: (jnp.minimum(bands[g], groups - 2), 0, l)
+    )
+    row = pl.BlockSpec((1, LANES), lambda g, l, bands: (0, g * wide + l))
+    return pl.pallas_call(
+        functools.partial(finish_kernel, count, wide),
+        grid_spec=pltpu.PrefetchScalarGridSpec(
+            num_scalar_prefetch=1,
+            grid=(groups, wide),
+            in_specs=[
+                block,
+                block,
+                far,
+                far,
+                pl.BlockSpec((count, 2, LANES), lambda g, l, bands: (0, 0, g * wide + l)),
+                row,
+                row,
+                row,
+            ],
+            out_specs=[
+                block,
+                block,
+                pl.BlockSpec((1, ROWS, LANES), lambda g, l, bands: (g, 0, l)),
+            ],
+        ),
+        out_shape=(
+            jax.ShapeDtypeStruct((rows, channels), x.dtype),
+            jax.ShapeDtypeStruct((rows, channels), x.dtype),
+            jax.ShapeDtypeStruct((groups, ROWS, channels // groups), jnp.float32),
+        ),
+        name="finish",
+    )(bands, x, c, far_x, far_c, ends, residue, decay, skip)
+
+
+def total_kernel(count, sums, total_ref, got, send, recv):
+    me = lax.axis_index("ctx")
+    greet(count, me)
+
+    def copy(step):
+        peer = lax.rem(me + step + 1, count)
+        return pltpu.make_async_remote_copy(
+            src_ref=sums.at[peer],
+            dst_ref=got.at[step],
+            send_sem=send.at[step],
+            recv_sem=recv.at[step],
+            device_id={"ctx": peer},
+            device_id_type=MESH,
+        )
+
+    for step in range(count - 1):
+        copy(step).start()
+    total = sums[me]
+    for step in range(count - 1):
+        copy(step).wait()
+        total = total + got[step]
+    total_ref[...] = total
+
+
+def total(count, sums):
+    inside = pl.BlockSpec(memory_space=pltpu.VMEM)
+    one = pltpu.SemaphoreType.DMA((count - 1,))
+    return pl.pallas_call(
+        functools.partial(total_kernel, count),
+        in_specs=[inside],
+        out_specs=inside,
+        out_shape=jax.ShapeDtypeStruct(sums.shape[1:], sums.dtype),
+        scratch_shapes=[
+            pltpu.VMEM((count - 1,) + sums.shape[1:], sums.dtype),
+            one,
+            one,
+        ],
+        compiler_params=pltpu.CompilerParams(collective_id=1, has_side_effects=True),
+        name="total",
+    )(sums)
+
+
+def banded(count, inputs, cotangent, residue, decay, skip_gain, band_blocks):
+    bands = band_blocks[0]
+    residue, decay, skip_gain = (part[None, :] for part in (residue, decay, skip_gain))
+    xs, cs, ends = pack(bands, inputs, cotangent, decay)
+    far_x, far_c, far_ends = swap(count, xs, cs, ends)
+    layer_out, input_grad, sums = finish(
+        count, bands, inputs, cotangent, far_x, far_c, far_ends, residue, decay, skip_gain
+    )
+    own = total(count, sums)
+    return (layer_out, input_grad, own[0], own[1], own[2])
+
+
+def local_body(count, inputs, cotangent, residue, decay, skip_gain, band_blocks):
+    rows, channels = inputs.shape
+    groups = band_blocks.shape[1]
+    fits = groups == count and count > 1 and rows % (2 * ROWS) == 0
+    if fits and channels % (groups * LANES) == 0:
+        return banded(count, inputs, cotangent, residue, decay, skip_gain, band_blocks)
+    return body(inputs, cotangent, residue, decay, skip_gain, band_blocks)
+
+
 def solution(mesh):
     placed = (P("ctx", "dp"), P("ctx", "dp"), P("dp"), P("dp"), P("dp"), P("dp", None))
     return jax.shard_map(
-        body,
+        functools.partial(local_body, mesh.shape["ctx"]),
         mesh=mesh,
         in_specs=placed,
         out_specs=(

time: 814 us -> 80.8 us (0.10); the launches traced: 799 us -> 80.3 us
  local copies, waits for them, and re-layouts: 458 us -> 1.38 us
  waiting for transfers between devices: 136 us -> 0 us
  other arithmetic: 135 us -> 0 us
  Pallas kernels: 0 us -> 78.2 us
  blocking collectives: 58.2 us -> 0 us
  starting transfers between devices: 9.93 us -> 0 us
    slice x106 -> x1, local copies, waits for them, and re-layouts: 264 us -> 1.38 us  [banded(): return (layer_out, input_grad, own[0], own[1], own[2])]
    all_to_all x2 -> x0, waiting for transfers between devices: 136 us -> none  [the longest x1 71.9 us: body(): lax.all_to_all(outgoing(back_carried, send_bwd, group_count, group_width)...]
    pad x36 -> x0, local copies, waits for them, and re-layouts: 93.8 us -> none  [local_scan(): return lax.associative_scan(compose, (factors, values), reverse=backward)[1]]
    pallas_call x0 -> x4, Pallas kernels: none -> 78.2 us  [the longest x1 52.1 us: swap(): pl.pallas_call(functools.partial(swap_kernel, count), in_specs=[anywhere]...]
    add x47 -> x0, other arithmetic: 67.1 us -> none  [the longest x27 38.2 us: compose(): earlier_pair[1] * later_pair[0] + later_pair[1]]
    all_gather x3 -> x0, blocking collectives: 41.3 us -> none  [prefix(): pieces = jax.tree.map(lambda part: lax.all_gather(part, axis), value)]
    rev x3 -> x0, local copies, waits for them, and re-layouts: 33.2 us -> none  [the longest x1 32.8 us: local_scan(): return lax.associative_scan(compose, (factors, values), reverse=backward)[1]]
    reshape x4 -> x0, local copies, waits for them, and re-layouts: 21.5 us -> none  [the longest x2 10.8 us: outgoing(): shaped = values.reshape(values.shape[0], group_count, group_width)]
  transfers between devices with their start and end apart: 2 -> 0, of which waited for: 2 -> 0; matrix products, arithmetic and copies ran while one was open for 5% -> 0% of each run, Pallas kernels for 0% -> 0%
where the time goes in v1:
time: 80.8 us; the launch traced here: 80.3 us
  Pallas kernels  78.2 us (97%)
  local copies, waits for them, and re-layouts  1.38 us (2%)
    pallas_call x1, Pallas kernels, swap(): pl.pallas_call(functools.partial(swap_kernel, count), in_specs=[anywhere]...  52.1 us
    pallas_call x1, Pallas kernels, finish(): pl.pallas_call(functools.partial(finish_kernel, count, wide), grid_spec=p...  13.4 us
    pallas_call x1, Pallas kernels, total(): pl.pallas_call(functools.partial(total_kernel, count), in_specs=[inside],...  6.88 us
    pallas_call x1, Pallas kernels, pack(): pl.pallas_call(pack_kernel, grid_spec=pltpu.PrefetchScalarGridSpec(num_sc...  5.89 us

profile of v1, /device:TPU:0, one launch (start us, length us, event | category | flops | bytes accessed | tf_op | source)
XLA Modules:
  0.0 80.3 jit_solution(12595421760089426890)
XLA Ops:
  0.6 5.9 %pack.1 = (bf16[4,1024,256]{2,1,0:T(8,128)(2,1)}, bf16[4,1024,256]{2,1,0:T(8,128)(2,1)}, f32[2,1024]{1,0:T(2,128)}) custom-call(s32[4]{0:T(128)} %bitcast.11, bf16[1024,1024]{1,0:T(8,128)(2,1)} %x_ref.3, bf16[1024,1024]{1,0:T(8,128)(2,1)} %c_ref.3, f32[1,1024]{1,0:T(1,128)} %bitcast.7), custom_call_target="tpu_custom_call" | custom-call | tf_op jit(solution)/shard_map/pack/pallas_call | solution.py:190
  6.5 52.1 %swap.1 = (bf16[3,1024,256]{2,1,0:T(8,128)(2,1)}, bf16[3,1024,256]{2,1,0:T(8,128)(2,1)}, f32[4,2,1024]{2,1,0:T(2,128)}) custom-call(bf16[4,1024,256]{2,1,0:T(8,128)(2,1)} %get-tuple-element.14.xs, bf16[4,1024,256]{2,1,0:T(8,128)(2,1)} %get-tuple-element.15.cs, f32[2,1024]{1,0:T(2,128)} %get-tuple-element.16.ends), custom_call_target="tpu_custom_call" | custom-call | tf_op jit(solution)/shard_map/swap/pallas_call | solution.py:270
  58.6 13.4 %finish.1 = (bf16[1024,1024]{1,0:T(8,128)(2,1)}, bf16[1024,1024]{1,0:T(8,128)(2,1)}, f32[4,8,256]{2,1,0:T(8,128)}) custom-call(s32[4]{0:T(128)} %bitcast.12, bf16[1024,1024]{1,0:T(8,128)(2,1)} %x_ref.3, bf16[1024,1024]{1,0:T(8,128)(2,1)} %c_ref.3, bf16[3,1024,256]{2,1,0:T(8,128)(2,1)} %get-tuple-element.17.far_x_ref, ...), custom_call_target="tpu_custom_call" | custom-call | tf_op jit(solution)/shard_map/finish/pallas_call | solution.py:405
  72.0 6.9 %total.1 = f32[8,256]{1,0:T(8,128)} custom-call(f32[4,8,256]{2,1,0:T(8,128)} %get-tuple-element.22.sums), custom_call_target="tpu_custom_call" | custom-call | tf_op jit(solution)/shard_map/total/pallas_call | solution.py:462
  78.9 1.4 %fusion = (f32[1,256]{1,0:T(1,128)}, f32[1,256]{1,0:T(1,128)}, f32[1,256]{1,0:T(1,128)}) fusion(f32[8,256]{1,0:T(8,128)} %total.1), kind=kLoop, calls=%fused_computation | loop fusion | bytes 6144 | tf_op jit(solution)/shard_map/slice | solution.py:486

commit v2 on v0

--- a/solution.py
+++ b/solution.py
@@ -1,6 +1,9 @@
+import functools
 import jax
 import jax.numpy as jnp
 from jax import lax
+from jax.experimental import pallas as pl
+from jax.experimental.pallas import tpu as pltpu
 from jax.sharding import PartitionSpec as P
 
 
@@ -125,10 +128,447 @@
     return (layer_out, input_grad, own_share[0], own_share[1], own_share[2])
 
 
+MESH = pl.DeviceIdType.MESH
+LANES = 128
+ROWS = 8
+PAIR = 2 * ROWS
+PIECES = 4
+UNROLL = 4
+
+
+def greet(count, me):
+    barrier = pltpu.get_barrier_semaphore()
+    for step in range(1, count):
+        pl.semaphore_signal(
+            barrier,
+            inc=1,
+            device_id={"ctx": lax.rem(me + step, count)},
+            device_id_type=MESH,
+        )
+    return lambda: pl.semaphore_wait(barrier, count - 1)
+
+
+def pieces_of(count, slot):
+    return PIECES if slot == count - 2 else 1
+
+
+def pair_at(step):
+    return pl.ds(pl.multiple_of(step * PAIR, PAIR), PAIR)
+
+
+def banded_kernel(
+    count,
+    bands,
+    x_hbm,
+    c_hbm,
+    residue_ref,
+    decay_ref,
+    skip_ref,
+    out_hbm,
+    grad_hbm,
+    total_ref,
+    x_all,
+    c_all,
+    xs,
+    cs,
+    far_x,
+    far_c,
+    ends,
+    far_ends,
+    outs,
+    grads,
+    sums,
+    got,
+    load_sem,
+    store_sem,
+    x_send,
+    x_recv,
+    c_send,
+    c_recv,
+    e_send,
+    e_recv,
+    s_send,
+    s_recv,
+):
+    me = lax.axis_index("ctx")
+    _, rows, width = x_all.shape
+    shape = (ROWS, width)
+    steps = rows // PAIR
+
+    def load(source, target, at, group):
+        lanes = pl.ds(group * width, width)
+        return pltpu.make_async_copy(
+            source.at[:, lanes], target.at[group], load_sem.at[at, group]
+        )
+
+    for at, (source, target) in enumerate(((x_hbm, x_all), (c_hbm, c_all))):
+        for group in range(count):
+            load(source, target, at, group).start()
+    all_here = greet(count, me)
+    groups = []
+    for slot in range(count):
+        group = jnp.int32(0)
+        for other in range(count):
+            group = jnp.where(bands[other] == slot, other, group)
+        groups.append(group)
+
+    def pack(whole, packed):
+        def turn(step, _):
+            at = pair_at(step)
+            for slot in range(count):
+                packed[slot, at, :] = whole[groups[slot], at, :]
+            return 0
+
+        lax.fori_loop(0, steps, turn, 0, unroll=UNROLL)
+
+    for at, (source, target, packed) in enumerate(((x_hbm, x_all, xs), (c_hbm, c_all, cs))):
+        for group in range(count):
+            load(source, target, at, group).wait()
+        pack(target, packed)
+
+    first_sem = [sum(pieces_of(count, s) for s in range(slot)) for slot in range(count)]
+
+    def x_copy(slot, piece):
+        size = rows // pieces_of(count, slot)
+        at = pl.ds(piece * size, size)
+        sem = first_sem[slot] + piece
+        return pltpu.make_async_remote_copy(
+            src_ref=xs.at[slot, at],
+            dst_ref=far_x.at[slot, at],
+            send_sem=x_send.at[sem],
+            recv_sem=x_recv.at[sem],
+            device_id={"ctx": lax.rem(me + slot + 1, count)},
+            device_id_type=MESH,
+        )
+
+    def c_copy(slot, piece):
+        size = rows // pieces_of(count, slot)
+        at = pl.ds(rows - (piece + 1) * size, size)
+        sem = first_sem[slot] + piece
+        return pltpu.make_async_remote_copy(
+            src_ref=cs.at[slot, at],
+            dst_ref=far_c.at[slot, at],
+            send_sem=c_send.at[sem],
+            recv_sem=c_recv.at[sem],
+            device_id={"ctx": lax.rem(me + count - slot - 1, count)},
+            device_id_type=MESH,
+        )
+
+    def small_copy(source, target, send, recv, step):
+        return pltpu.make_async_remote_copy(
+            src_ref=source,
+            dst_ref=target,
+            send_sem=send.at[step],
+            recv_sem=recv.at[step],
+            device_id={"ctx": lax.rem(me + step + 1, count)},
+            device_id_type=MESH,
+        )
+
+    def end_copy(step):
+        return small_copy(ends, far_ends.at[me], e_send, e_recv, step)
+
+    def share_copy(slot, step):
+        at = slot * (count - 1) + step
+        return pltpu.make_async_remote_copy(
+            src_ref=sums.at[slot],
+            dst_ref=got.at[step, slot],
+            send_sem=s_send.at[at],
+            recv_sem=s_recv.at[at],
+            device_id={"ctx": lax.rem(me + step + 1, count)},
+            device_id_type=MESH,
+        )
+
+    def store(slot, piece, backward):
+        pieces = pieces_of(count, slot)
+        size = rows // pieces
+        source, target = (grads, grad_hbm) if backward else (outs, out_hbm)
+        at = pl.ds(rows - (piece + 1) * size if backward else piece * size, size)
+        sem = store_sem.at[int(backward), first_sem[slot] + piece]
+        return pltpu.make_async_copy(source.at[slot, at], target.at[slot, at], sem)
+
+    def send(slot):
+        for piece in range(pieces_of(count, slot)):
+            pl.when(me + slot + 1 < count)(lambda: x_copy(slot, piece).start())
+            pl.when(me >= slot + 1)(lambda: c_copy(slot, piece).start())
+
+    all_here()
+    send(0)
+
+    level = lax.broadcasted_iota(jnp.int32, shape, 0)
+    depth = level.astype(jnp.float32)
+    zero = jnp.zeros(shape, jnp.float32)
+    for slot in range(count):
+        rate = decay_ref[groups[slot]]
+        leap_pair = jnp.broadcast_to(jnp.exp(-rate * PAIR), shape)
+
+        def turn(step, held):
+            ahead = xs[slot, pair_at(step), :].astype(jnp.float32)
+            back = cs[slot, pair_at(steps - 1 - step), :].astype(jnp.float32)
+            parts = (ahead[:ROWS], ahead[ROWS:], back[:ROWS], back[ROWS:])
+            return tuple(old * leap_pair + new for old, new in zip(held, parts))
+
+        upper, lower, back_upper, back_lower = lax.fori_loop(
+            0, steps, turn, (zero,) * 4, unroll=UNROLL
+        )
+        last = upper * jnp.exp(-rate * (PAIR - 1 - depth)) + lower * jnp.exp(
+            -rate * (ROWS - 1 - depth)
+        )
+        first = back_upper * jnp.exp(-rate * depth) + back_lower * jnp.exp(
+            -rate * (ROWS + depth)
+        )
+        ends[slot, 0:1, :] = jnp.sum(last, axis=0, keepdims=True)
+        ends[slot, 1:2, :] = jnp.sum(first, axis=0, keepdims=True)
+    for step in range(count - 1):
+        end_copy(step).start()
+    for slot in range(1, count - 1):
+        send(slot)
+    for step in range(count - 1):
+        end_copy(step).wait()
+
+    def scan(tile, hops):
+        for hop, factor in hops:
+            tile = tile + factor * pltpu.roll(tile, hop, 0)
+        return tile
+
+    def work(slot):
+        band = slot + 1
+        has_before = me >= band
+        has_after = me + band < count
+        reach = slot < count - 1
+        rate = decay_ref[groups[slot]]
+        residue_row = residue_ref[groups[slot]]
+        carry = jnp.zeros((1, width), jnp.float32)
+        back_carry = carry
+        for other in range(count):
+            apart = me - 1 - other
+            kept = jnp.logical_and(apart >= 0, apart < band)
+            factor = jnp.exp(-rate * (jnp.maximum(apart, 0) * rows).astype(jnp.float32))
+            carry = carry + jnp.where(kept, factor * far_ends[other, slot, 0:1, :], 0.0)
+            apart = other - me - 1
+            kept = jnp.logical_and(apart >= 0, apart < band)
+            factor = jnp.exp(-rate * (jnp.maximum(apart, 0) * rows).astype(jnp.float32))
+            back_carry = back_carry + jnp.where(
+                kept, factor * far_ends[other, slot, 1:2, :], 0.0
+            )
+        tail = jnp.broadcast_to(jnp.exp(-rate * float(band * rows)), shape)
+        leap = jnp.broadcast_to(jnp.exp(-rate * ROWS), shape)
+        residue = jnp.broadcast_to(residue_row, shape)
+        skip = jnp.broadcast_to(skip_ref[groups[slot]], shape)
+        lead = jnp.exp(-rate * (depth + 1.0))
+        trail = jnp.exp(-rate * (ROWS - depth))
+        fwd = [
+            (hop, jnp.where(level >= hop, jnp.exp(-rate * hop), 0.0)) for hop in (1, 2, 4)
+        ]
+        bwd = [
+            (ROWS - hop, jnp.where(level < ROWS - hop, jnp.exp(-rate * hop), 0.0))
+            for hop in (1, 2, 4)
+        ]
+
+        def forward(step, state):
+            carry, s_skip, s_w, s_tw = state
+            at = pair_at(step)
+            base = (step * PAIR).astype(jnp.float32)
+            x = xs[slot, at, :].astype(jnp.float32)
+            c = cs[slot, at, :].astype(jnp.float32)
+            if reach:
+                far = far_x[slot, at, :].astype(jnp.float32)
+            made = []
+            for half in range(2):
+                part = slice(half * ROWS, (half + 1) * ROWS)
+                fresh = x[part]
+                if reach:
+                    fresh = fresh - jnp.where(has_before, tail * far[part], 0.0)
+                local = scan(fresh, fwd)
+                truncated = local + lead * carry
+                carry = leap * carry + jnp.broadcast_to(local[ROWS - 1 :], shape)
+                made.append(skip * x[part] + residue * truncated)
+                w = c[part] * truncated
+                s_skip = s_skip + x[part] * c[part]
+                s_w = s_w + w
+                s_tw = s_tw + (base + half * ROWS) * w
+            outs[slot, at, :] = jnp.concatenate(made, axis=0).astype(outs.dtype)
+            return carry, s_skip, s_w, s_tw
+
+        def backward(step, state):
+            carry, s_v, s_tv = state
+            at = pair_at(steps - 1 - step)
+            base = ((steps - 1 - step) * PAIR).astype(jnp.float32)
+            x = xs[slot, at, :].astype(jnp.float32)
+            c = cs[slot, at, :].astype(jnp.float32)
+            if reach:
+                far = far_c[slot, at, :].astype(jnp.float32)
+            made = [None, None]
+            for half in (1, 0):
+                part = slice(half * ROWS, (half + 1) * ROWS)
+                fresh = c[part]
+                if reach:
+                    fresh = fresh - jnp.where(has_after, tail * far[part], 0.0)
+                local = scan(fresh, bwd)
+                truncated = local + trail * carry
+                carry = leap * carry + jnp.broadcast_to(local[:1], shape)
+                made[half] = skip * c[part] + residue * truncated
+                v = x[part] * truncated
+                s_v = s_v + v
+                s_tv = s_tv + (base + half * ROWS) * v
+            grads[slot, at, :] = jnp.concatenate(made, axis=0).astype(grads.dtype)
+            return carry, s_v, s_tv
+
+        ahead = (jnp.broadcast_to(carry, shape), zero, zero, zero)
+        back = (jnp.broadcast_to(back_carry, shape), zero, zero)
+        pieces = pieces_of(count, slot)
+        for piece in range(pieces):
+            span = (piece * steps // pieces, (piece + 1) * steps // pieces)
+            if reach:
+                pl.when(has_before)(lambda: x_copy(slot, piece).wait_recv())
+            ahead = lax.fori_loop(*span, forward, ahead, unroll=UNROLL)
+            store(slot, piece, False).start()
+            if reach:
+                pl.when(has_after)(lambda: c_copy(slot, piece).wait_recv())
+            back = lax.fori_loop(*span, backward, back, unroll=UNROLL)
+            store(slot, piece, True).start()
+        _, s_skip, s_w, s_tw = ahead
+        _, s_v, s_tv = back
+        offset = depth + (me * rows).astype(jnp.float32)
+        moment = (s_tw - s_tv) + offset * (s_w - s_v)
+        sums[slot, 0:1, :] = jnp.sum(s_skip, axis=0, keepdims=True)
+        sums[slot, 1:2, :] = jnp.sum(s_w, axis=0, keepdims=True)
+        sums[slot, 2:3, :] = (
+            -rate * residue_row * jnp.sum(moment, axis=0, keepdims=True)
+        )
+        for step in range(count - 1):
+            share_copy(slot, step).start()
+
+    sums[...] = jnp.zeros_like(sums)
+    work(count - 1)
+    for slot in range(count - 1):
+        work(slot)
+
+    for slot in range(count):
+        for piece in range(pieces_of(count, slot)):
+            store(slot, piece, False).wait()
+            store(slot, piece, True).wait()
+    for slot in range(count):
+        total = sums[slot]
+        for step in range(count - 1):
+            share_copy(slot, step).wait()
+            total = total + got[step, slot]
+        total_ref[slot] = total
+    for slot in range(count - 1):
+        for piece in range(pieces_of(count, slot)):
+            pl.when(me + slot + 1 < count)(lambda: x_copy(slot, piece).wait_send())
+            pl.when(me >= slot + 1)(lambda: c_copy(slot, piece).wait_send())
+
+
+def place_kernel(bands, out, grad, total, out_ref, grad_ref, skip_ref, residue_ref, decay_ref):
+    out_ref[...] = out[0]
+    grad_ref[...] = grad[0]
+    own = total[bands[lax.axis_index("ctx")]]
+    skip_ref[...] = own[0:1]
+    residue_ref[...] = own[1:2]
+    decay_ref[...] = own[2:3]
+
+
+def place(bands, outs, grads, totals):
+    count, rows, width = outs.shape
+    slot = pl.BlockSpec((1, rows // 2, width), lambda g, r, bands: (bands[g], r, 0))
+    block = pl.BlockSpec((rows // 2, width), lambda g, r, bands: (r, g))
+    one = pl.BlockSpec((1, width), lambda g, r, bands: (0, 0))
+    whole = jax.ShapeDtypeStruct((rows, count * width), outs.dtype)
+    small = jax.ShapeDtypeStruct((1, width), totals.dtype)
+    return pl.pallas_call(
+        place_kernel,
+        grid_spec=pltpu.PrefetchScalarGridSpec(
+            num_scalar_prefetch=1,
+            grid=(count, 2),
+            in_specs=[
+                slot,
+                slot,
+                pl.BlockSpec(totals.shape, lambda g, r, bands: (0, 0, 0)),
+            ],
+            out_specs=[block, block, one, one, one],
+        ),
+        out_shape=(whole, whole, small, small, small),
+        name="place",
+    )(bands, outs, grads, totals)
+
+
+def banded(count, inputs, cotangent, residue, decay, skip_gain, band_blocks):
+    rows, channels = inputs.shape
+    width = channels // count
+    bands = band_blocks[0]
+    anywhere = pl.BlockSpec(memory_space=pl.ANY)
+    inside = pl.BlockSpec(memory_space=pltpu.VMEM)
+    flows = sum(pieces_of(count, slot) for slot in range(count))
+    many = pltpu.SemaphoreType.DMA((flows,))
+    few = pltpu.SemaphoreType.DMA((count - 1,))
+    some = pltpu.SemaphoreType.DMA((count * (count - 1),))
+    packed = pltpu.VMEM((count, rows, width), inputs.dtype)
+    far = pltpu.VMEM((count - 1, rows, width), inputs.dtype)
+    outs, grads, totals = pl.pallas_call(
+        functools.partial(banded_kernel, count),
+        in_specs=[
+            pl.BlockSpec(memory_space=pltpu.SMEM),
+            anywhere,
+            anywhere,
+            inside,
+            inside,
+            inside,
+        ],
+        out_specs=[anywhere, anywhere, inside],
+        out_shape=(
+            jax.ShapeDtypeStruct((count, rows, width), inputs.dtype),
+            jax.ShapeDtypeStruct((count, rows, width), inputs.dtype),
+            jax.ShapeDtypeStruct((count, ROWS // 2, width), jnp.float32),
+        ),
+        scratch_shapes=[
+            packed,
+            packed,
+            packed,
+            packed,
+            far,
+            far,
+            pltpu.VMEM((count, 2, width), jnp.float32),
+            pltpu.VMEM((count, count, 2, width), jnp.float32),
+            packed,
+            packed,
+            pltpu.VMEM((count, ROWS // 2, width), jnp.float32),
+            pltpu.VMEM((count - 1, count, ROWS // 2, width), jnp.float32),
+            pltpu.SemaphoreType.DMA((2, count)),
+            pltpu.SemaphoreType.DMA((2, flows)),
+            many,
+            many,
+            many,
+            many,
+            few,
+            few,
+            some,
+            some,
+        ],
+        compiler_params=pltpu.CompilerParams(collective_id=0, has_side_effects=True),
+        name="banded",
+    )(
+        bands,
+        inputs,
+        cotangent,
+        *(part.reshape(count, 1, width) for part in (residue, decay, skip_gain)),
+    )
+    layer_out, input_grad, *sums = place(bands, outs, grads, totals)
+    return (layer_out, input_grad, *(part.reshape(width) for part in sums))
+
+
+def local_body(count, inputs, cotangent, residue, decay, skip_gain, band_blocks):
+    rows, channels = inputs.shape
+    groups = band_blocks.shape[1]
+    fits = groups == count and count > 1 and rows % (PAIR * PIECES) == 0
+    if fits and channels % (groups * LANES) == 0:
+        return banded(count, inputs, cotangent, residue, decay, skip_gain, band_blocks)
+    return body(inputs, cotangent, residue, decay, skip_gain, band_blocks)
+
+
 def solution(mesh):
     placed = (P("ctx", "dp"), P("ctx", "dp"), P("dp"), P("dp"), P("dp"), P("dp", None))
     return jax.shard_map(
-        body,
+        functools.partial(local_body, mesh.shape["ctx"]),
         mesh=mesh,
         in_specs=placed,
         out_specs=(

time: 814 us -> 71.6 us (0.09); the launches traced: 799 us -> 71.3 us
  local copies, waits for them, and re-layouts: 458 us -> 0 us
  waiting for transfers between devices: 136 us -> 0 us
  other arithmetic: 135 us -> 0 us
  Pallas kernels: 0 us -> 70.7 us
  blocking collectives: 58.2 us -> 0 us
  starting transfers between devices: 9.93 us -> 0 us
    slice x106 -> x0, local copies, waits for them, and re-layouts: 264 us -> none  [the longest x105 264 us: local_scan(): return lax.associative_scan(compose, (factors, values), reverse=backward)[1]]
    all_to_all x2 -> x0, waiting for transfers between devices: 136 us -> none  [the longest x1 71.9 us: body(): lax.all_to_all(outgoing(back_carried, send_bwd, group_count, group_width)...]
    pad x36 -> x0, local copies, waits for them, and re-layouts: 93.8 us -> none  [local_scan(): return lax.associative_scan(compose, (factors, values), reverse=backward)[1]]
    pallas_call x0 -> x2, Pallas kernels: none -> 70.7 us  [the longest x1 63.4 us: banded(): pl.pallas_call(functools.partial(banded_kernel, count), in_specs=[pl.Bloc...]
    add x47 -> x0, other arithmetic: 67.1 us -> none  [the longest x27 38.2 us: compose(): earlier_pair[1] * later_pair[0] + later_pair[1]]
    all_gather x3 -> x0, blocking collectives: 41.3 us -> none  [prefix(): pieces = jax.tree.map(lambda part: lax.all_gather(part, axis), value)]
    rev x3 -> x0, local copies, waits for them, and re-layouts: 33.2 us -> none  [the longest x1 32.8 us: local_scan(): return lax.associative_scan(compose, (factors, values), reverse=backward)[1]]
    reshape x4 -> x0, local copies, waits for them, and re-layouts: 21.5 us -> none  [the longest x2 10.8 us: outgoing(): shaped = values.reshape(values.shape[0], group_count, group_width)]
  transfers between devices with their start and end apart: 2 -> 0, of which waited for: 2 -> 0; matrix products, arithmetic and copies ran while one was open for 5% -> 0% of each run, Pallas kernels for 0% -> 0%
where the time goes in v2:
time: 71.6 us; the launch traced here: 71.3 us
  Pallas kernels  70.7 us (99%)
    pallas_call x1, Pallas kernels, banded(): pl.pallas_call(functools.partial(banded_kernel, count), in_specs=[pl.Bloc...  63.4 us
    pallas_call x1, Pallas kernels, place(): pl.pallas_call(place_kernel, grid_spec=pltpu.PrefetchScalarGridSpec(num_s...  7.26 us

profile of v2, /device:TPU:0, one launch (start us, length us, event | category | flops | bytes accessed | tf_op | source)
XLA Modules:
  0.0 71.3 jit_solution(6042416565929841511)
XLA Ops:
  0.6 63.4 %banded.1 = (bf16[4,1024,256]{2,1,0:T(8,128)(2,1)}, bf16[4,1024,256]{2,1,0:T(8,128)(2,1)}, f32[4,4,256]{2,1,0:T(4,128)}) custom-call(s32[4]{0:T(128)} %bitcast.10, bf16[1024,1024]{1,0:T(8,128)(2,1)} %x_hbm.1, bf16[1024,1024]{1,0:T(8,128)(2,1)} %c_hbm.1, f32[4,1,256]{2,1,0:T(1,128)} %bitcast.7, f32[4,1,256]{2,1,0:T(1,128)} %bitcast.8, f32[4,1,256]{2,1,0:T(1,128)} %bitcast.9), custom_call_target="tpu_custom_call" | custom-call | tf_op jit(solution)/shard_map/banded/pallas_call | solution.py:507
  64.0 7.3 %place.1 = (bf16[1024,1024]{1,0:T(8,128)(2,1)}, bf16[1024,1024]{1,0:T(8,128)(2,1)}, f32[1,256]{1,0:T(1,128)}, f32[1,256]{1,0:T(1,128)}, f32[1,256]{1,0:T(1,128)}) custom-call(s32[4]{0:T(128)} %bitcast.11, bf16[4,1024,256]{2,1,0:T(8,128)(2,1)} %get-tuple-element.13.out, bf16[4,1024,256]{2,1,0:T(8,128)(2,1)} %get-tuple-element.14.grad, ...), custom_call_target="tpu_custom_call" | custom-call | tf_op jit(solution)/shard_map/place/pallas_call | solution.py:478

commit v3 on v2

--- a/solution.py
+++ b/solution.py
@@ -390,7 +390,7 @@
             return carry, s_skip, s_w, s_tw
 
         def backward(step, state):
-            carry, s_v, s_tv = state
+            carry, unused, s_v, s_tv = state
             at = pair_at(steps - 1 - step)
             base = ((steps - 1 - step) * PAIR).astype(jnp.float32)
             x = xs[slot, at, :].astype(jnp.float32)
@@ -411,23 +411,43 @@
                 s_v = s_v + v
                 s_tv = s_tv + (base + half * ROWS) * v
             grads[slot, at, :] = jnp.concatenate(made, axis=0).astype(grads.dtype)
-            return carry, s_v, s_tv
+            return carry, unused, s_v, s_tv
 
         ahead = (jnp.broadcast_to(carry, shape), zero, zero, zero)
-        back = (jnp.broadcast_to(back_carry, shape), zero, zero)
+        back = (jnp.broadcast_to(back_carry, shape), zero, zero, zero)
         pieces = pieces_of(count, slot)
-        for piece in range(pieces):
-            span = (piece * steps // pieces, (piece + 1) * steps // pieces)
-            if reach:
-                pl.when(has_before)(lambda: x_copy(slot, piece).wait_recv())
-            ahead = lax.fori_loop(*span, forward, ahead, unroll=UNROLL)
-            store(slot, piece, False).start()
-            if reach:
-                pl.when(has_after)(lambda: c_copy(slot, piece).wait_recv())
-            back = lax.fori_loop(*span, backward, back, unroll=UNROLL)
-            store(slot, piece, True).start()
+
+        def run(backwards, state):
+            for piece in range(pieces):
+                span = (piece * steps // pieces, (piece + 1) * steps // pieces)
+                if reach and backwards:
+                    pl.when(has_after)(lambda: c_copy(slot, piece).wait_recv())
+                elif reach:
+                    pl.when(has_before)(lambda: x_copy(slot, piece).wait_recv())
+                turn = backward if backwards else forward
+                state = lax.fori_loop(*span, turn, state, unroll=UNROLL)
+                store(slot, piece, backwards).start()
+            return state
+
+        if not reach or 2 * band < count:
+            ahead = run(False, ahead)
+            back = run(True, back)
+            close(slot, rate, residue_row, ahead, back)
+            return None
+        ready = lax.cond(has_after, lambda: run(False, ahead), lambda: run(True, back))
+
+        def rest():
+            late = lax.cond(has_after, lambda: run(True, back), lambda: run(False, ahead))
+            pick = lambda left, right: tuple(
+                jnp.where(has_after, one, two) for one, two in zip(left, right)
+            )
+            close(slot, rate, residue_row, pick(ready, late), pick(late, ready))
+
+        return rest
+
+    def close(slot, rate, residue_row, ahead, back):
         _, s_skip, s_w, s_tw = ahead
-        _, s_v, s_tv = back
+        _, _, s_v, s_tv = back
         offset = depth + (me * rows).astype(jnp.float32)
         moment = (s_tw - s_tv) + offset * (s_w - s_v)
         sums[slot, 0:1, :] = jnp.sum(s_skip, axis=0, keepdims=True)
@@ -440,8 +460,10 @@
 
     sums[...] = jnp.zeros_like(sums)
     work(count - 1)
-    for slot in range(count - 1):
-        work(slot)
+    pending = [work(slot) for slot in range(count - 1)]
+    for rest in pending:
+        if rest is not None:
+            rest()
 
     for slot in range(count):
         for piece in range(pieces_of(count, slot)):
@@ -470,8 +492,8 @@
 
 def place(bands, outs, grads, totals):
     count, rows, width = outs.shape
-    slot = pl.BlockSpec((1, rows // 2, width), lambda g, r, bands: (bands[g], r, 0))
-    block = pl.BlockSpec((rows // 2, width), lambda g, r, bands: (r, g))
+    slot = pl.BlockSpec((1, rows, width), lambda g, r, bands: (bands[g], r, 0))
+    block = pl.BlockSpec((rows, width), lambda g, r, bands: (r, g))
     one = pl.BlockSpec((1, width), lambda g, r, bands: (0, 0))
     whole = jax.ShapeDtypeStruct((rows, count * width), outs.dtype)
     small = jax.ShapeDtypeStruct((1, width), totals.dtype)
@@ -479,7 +501,7 @@
         place_kernel,
         grid_spec=pltpu.PrefetchScalarGridSpec(
             num_scalar_prefetch=1,
-            grid=(count, 2),
+            grid=(count, 1),
             in_specs=[
                 slot,
                 slot,

time: 71.6 us -> 67.5 us (0.943)
  Pallas kernels: 70.7 us -> 66.6 us
    pallas_call x1, Pallas kernels: 63.4 us -> 61.2 us  [banded(): pl.pallas_call(functools.partial(banded_kernel, count), in_specs=[pl.Bloc...]
    pallas_call x1, Pallas kernels: 7.26 us -> 5.39 us  [place(): pl.pallas_call(place_kernel, grid_spec=pltpu.PrefetchScalarGridSpec(num_s...]
where the time goes in v3:
time: 67.5 us; the launch traced here: 67.3 us
  Pallas kernels  66.6 us (99%)
    pallas_call x1, Pallas kernels, banded(): pl.pallas_call(functools.partial(banded_kernel, count), in_specs=[pl.Bloc...  61.2 us
    pallas_call x1, Pallas kernels, place(): pl.pallas_call(place_kernel, grid_spec=pltpu.PrefetchScalarGridSpec(num_s...  5.39 us

profile of v3, /device:TPU:0, one launch (start us, length us, event | category | flops | bytes accessed | tf_op | source)
XLA Modules:
  0.0 67.3 jit_solution(6506352060800939424)
XLA Ops:
  0.6 61.2 %banded.1 = (bf16[4,1024,256]{2,1,0:T(8,128)(2,1)}, bf16[4,1024,256]{2,1,0:T(8,128)(2,1)}, f32[4,4,256]{2,1,0:T(4,128)}) custom-call(s32[4]{0:T(128)} %bitcast.10, bf16[1024,1024]{1,0:T(8,128)(2,1)} %x_hbm.1, bf16[1024,1024]{1,0:T(8,128)(2,1)} %c_hbm.1, f32[4,1,256]{2,1,0:T(1,128)} %bitcast.7, f32[4,1,256]{2,1,0:T(1,128)} %bitcast.8, f32[4,1,256]{2,1,0:T(1,128)} %bitcast.9), custom_call_target="tpu_custom_call" | custom-call | tf_op jit(solution)/shard_map/banded/pallas_call | solution.py:529
  61.9 5.4 %place.1 = (bf16[1024,1024]{1,0:T(8,128)(2,1)}, bf16[1024,1024]{1,0:T(8,128)(2,1)}, f32[1,256]{1,0:T(1,128)}, f32[1,256]{1,0:T(1,128)}, f32[1,256]{1,0:T(1,128)}) custom-call(s32[4]{0:T(128)} %bitcast.11, bf16[4,1024,256]{2,1,0:T(8,128)(2,1)} %get-tuple-element.13.out, bf16[4,1024,256]{2,1,0:T(8,128)(2,1)} %get-tuple-element.14.grad, ...), custom_call_target="tpu_custom_call" | custom-call | tf_op jit(solution)/shard_map/place/pallas_call | solution.py:500
